TPU v7x, 32 devices: a whole 2x2x4 slice. The times are simulated.
32 devices in a mesh: fsdp: 8 (over z, y), tp: 4 (over x, core).
Axes of the slice: x: 2, y: 2, z: 4, core: 2. Of those that a mesh axis runs over, the one named last changes fastest.
Arguments:
- layer_input: bfloat16 [8192, 768], P(('fsdp', 'tp')), may hold values from -12 to 12
- out_cotangent: bfloat16 [8192, 768], P(('fsdp', 'tp')), may hold values from -12 to 12
- segments: int32 [8, 1024], P('fsdp'), may hold values from 0 to 3, never falling along the last dimension, each value on 1 to 512 neighbouring positions
- norm_gain: float32 [768], replicated, may hold values from 0.5 to 1.5
- norm_bias: float32 [768], replicated, may hold values from -3 to 3
- qkv_weight: bfloat16 [768, 2304], P('fsdp', 'tp'), may hold values from -20 to 20
- qkv_bias: float32 [2304], P('tp'), may hold values from -3 to 3
- out_weight: bfloat16 [768, 768], P('tp', 'fsdp'), may hold values from -0.875 to 0.875
- out_bias: float32 [768], replicated, may hold values from -3 to 3
- up_weight: bfloat16 [768, 3072], P('fsdp', 'tp'), may hold values from -0.21875 to 0.21875
- up_bias: float32 [3072], P('tp'), may hold values from -3 to 3
- down_weight: bfloat16 [3072, 768], P('tp', 'fsdp'), may hold values from -0.109375 to 0.109375
- down_bias: float32 [768], replicated, may hold values from -3 to 3
Outputs:
- layer_output: bfloat16 [8192, 768], P(('fsdp', 'tp'))
- input_grad: bfloat16 [8192, 768], P(('fsdp', 'tp'))
- norm_gain_grad: float32 [768], replicated
- norm_bias_grad: float32 [768], replicated
- qkv_weight_grad: float32 [768, 2304], P('fsdp', 'tp')
- qkv_bias_grad: float32 [2304], P('tp')
- out_weight_grad: float32 [768, 768], P('tp', 'fsdp')
- out_bias_grad: float32 [768], replicated
- up_weight_grad: float32 [768, 3072], P('fsdp', 'tp')
- up_bias_grad: float32 [3072], P('tp')
- down_weight_grad: float32 [3072, 768], P('tp', 'fsdp')
- down_bias_grad: float32 [768], replicated
Inputs may be any that keep to these rules, and one draw needn't show every extreme that they name: `segments`: each row is one sequence of 1024 tokens; its numbers name documents, never fall along the row, and each document spans 1 to 512 tokens, one exactly 512.
All inputs are finite; a program needn't handle non-finite values.
Results may differ from a plain program's by a relative error of at most 0.01.
Values may be sent and summed in bfloat16 or wider, within the bound.
A program may use at most 128 MiB of HBM per device.

v0:
```python
import jax
import jax.numpy as jnp
from jax import lax
from jax.sharding import PartitionSpec as P

HEAD_DIM = 64
ROT = 16
EPSILON = 1e-05
ROTARY_BASE = 10000.0


def layer_norm(values, gain, shift):
    center = values - jnp.mean(values, axis=-1, keepdims=True)
    spread = jnp.mean(center * center, axis=-1, keepdims=True)
    inverse = lax.rsqrt(spread + EPSILON)
    normed = center * inverse
    return (normed, inverse, normed * gain + shift)


def gelu_value(pre_act):
    return 0.5 * pre_act * (1.0 + lax.erf(pre_act * 0.7071067811865476))


def gelu_slope(pre_act):
    return (
        0.5 * (1.0 + lax.erf(pre_act * 0.7071067811865476))
        + pre_act * jnp.exp(-0.5 * pre_act * pre_act) * 0.3989422804014327
    )


def positions_of(segment_row):
    length = segment_row.shape[0]
    counter = jnp.arange(length, dtype=jnp.int32)
    is_start = jnp.concatenate(
        [jnp.ones((1,), dtype=jnp.bool_), segment_row[1:] != segment_row[:-1]]
    )
    starts = lax.cummax(jnp.where(is_start, counter, jnp.zeros_like(counter)), axis=0)
    return counter - starts


def rotary_tables(positions):
    halves = ROT // 2
    inverse_freq = ROTARY_BASE ** (-(jnp.arange(halves, dtype=jnp.float32) * 2.0) / ROT)
    angles = positions.astype(jnp.float32)[:, None] * inverse_freq[None, :]
    cos_table = jnp.cos(angles)
    sin_table = jnp.sin(angles)
    return (
        jnp.concatenate([cos_table, cos_table], axis=-1),
        jnp.concatenate([sin_table, sin_table], axis=-1),
    )


def rotate(tensor, cos_table, sin_table):
    halves = ROT // 2
    turned_part = tensor[..., :ROT]
    turned = jnp.concatenate([-turned_part[..., halves:], turned_part[..., :halves]], axis=-1)
    spun = turned_part * cos_table[:, None, :] + turned * sin_table[:, None, :]
    return jnp.concatenate([spun, tensor[..., ROT:]], axis=-1)


def unrotate(grad_in, cos_table, sin_table):
    halves = ROT // 2
    turned_part = grad_in[..., :ROT]
    scaled = turned_part * sin_table[:, None, :]
    back = jnp.concatenate([scaled[..., halves:], -scaled[..., :halves]], axis=-1)
    return jnp.concatenate(
        [turned_part * cos_table[:, None, :] + back, grad_in[..., ROT:]], axis=-1
    )


def cross_rows(left, right):
    return lax.dot_general(
        left, right, (((0,), (0,)), ((), ())), preferred_element_type=jnp.float32
    )


def cross_cols(left, right):
    return lax.dot_general(
        left, right, (((1,), (1,)), ((), ())), preferred_element_type=jnp.float32
    )


def block_scores(queries, keys_in, segment_row, first_row, last_row, score_scale):
    counter = jnp.arange(last_row, dtype=jnp.int32)
    allowed = (segment_row[first_row:last_row, None] == segment_row[None, :last_row]) & (
        counter[first_row:last_row, None] >= counter[None, :last_row]
    )
    scores = cross_cols(queries[first_row:last_row], keys_in[:last_row]) * score_scale
    return jnp.where(allowed, scores, -jnp.inf)


def head_forward(queries, keys_in, values_in, segment_row, score_scale):
    length = queries.shape[0]
    span = min(512, length)
    mixed_parts = []
    total_parts = []
    for first_row in range(0, length, span):
        last_row = min(first_row + span, length)
        scores = block_scores(queries, keys_in, segment_row, first_row, last_row, score_scale)
        highest = jnp.max(scores, axis=-1, keepdims=True)
        log_total = highest + jnp.log(jnp.sum(jnp.exp(scores - highest), axis=-1, keepdims=True))
        weights = jnp.exp(scores - log_total).astype(jnp.bfloat16)
        mixed_parts.append(
            jnp.dot(weights, values_in[:last_row], preferred_element_type=jnp.float32).astype(
                jnp.bfloat16
            )
        )
        total_parts.append(log_total)
    return (jnp.concatenate(mixed_parts, axis=0), jnp.concatenate(total_parts, axis=0))


def head_backward(
    queries, keys_in, values_in, mixed, grad_mixed, log_total, segment_row, score_scale
):
    length = queries.shape[0]
    span = min(512, length)
    delta = jnp.sum(
        grad_mixed.astype(jnp.float32) * mixed.astype(jnp.float32), axis=-1, keepdims=True
    )
    grad_keys = jnp.zeros(keys_in.shape, jnp.float32)
    grad_values = jnp.zeros(values_in.shape, jnp.float32)
    query_parts = []
    for first_row in range(0, length, span):
        last_row = min(first_row + span, length)
        padding = ((0, length - last_row), (0, 0))
        scores = block_scores(queries, keys_in, segment_row, first_row, last_row, score_scale)
        probs = jnp.exp(scores - log_total[first_row:last_row])
        weights = probs.astype(jnp.bfloat16)
        grad_rows = grad_mixed[first_row:last_row]
        grad_values = grad_values + jnp.pad(cross_rows(weights, grad_rows), padding)
        grad_probs = cross_cols(grad_rows, values_in[:last_row])
        grad_scores = (probs * (grad_probs - delta[first_row:last_row]) * score_scale).astype(
            jnp.bfloat16
        )
        query_parts.append(
            jnp.dot(grad_scores, keys_in[:last_row], preferred_element_type=jnp.float32)
        )
        grad_keys = grad_keys + jnp.pad(
            cross_rows(grad_scores, queries[first_row:last_row]), padding
        )
    return (jnp.concatenate(query_parts, axis=0), grad_keys, grad_values)


def body(
    layer_input,
    out_cotangent,
    segments,
    norm_gain,
    norm_bias,
    qkv_weight,
    qkv_bias,
    out_weight,
    out_bias,
    up_weight,
    up_bias,
    down_weight,
    down_bias,
):
    score_scale = HEAD_DIM ** (-0.5)
    own_rows = layer_input.astype(jnp.float32)
    normed, inverse, shifted = layer_norm(own_rows, norm_gain, norm_bias)
    features = lax.all_gather(shifted.astype(jnp.bfloat16), "tp", axis=0, tiled=True)
    length = features.shape[0]
    full_qkv, full_out, full_up, full_down = (
        lax.all_gather(qkv_weight, "fsdp", axis=0, tiled=True),
        lax.all_gather(out_weight, "fsdp", axis=1, tiled=True),
        lax.all_gather(up_weight, "fsdp", axis=0, tiled=True),
        lax.all_gather(down_weight, "fsdp", axis=1, tiled=True),
    )
    local_heads = full_qkv.shape[1] // (3 * HEAD_DIM)
    segment_row = segments[0]
    cos_table, sin_table = rotary_tables(positions_of(segment_row))
    packed = (jnp.dot(features, full_qkv, preferred_element_type=jnp.float32) + qkv_bias).reshape(
        length, local_heads, 3, HEAD_DIM
    )
    queries = rotate(packed[:, :, 0], cos_table, sin_table).astype(jnp.bfloat16).transpose(1, 0, 2)
    keys_all = rotate(packed[:, :, 1], cos_table, sin_table).astype(jnp.bfloat16).transpose(1, 0, 2)
    values_all = packed[:, :, 2].astype(jnp.bfloat16).transpose(1, 0, 2)

    def forward_head(member):
        return head_forward(member[0], member[1], member[2], segment_row, score_scale)

    mixed, log_total = lax.map(forward_head, (queries, keys_all, values_all))
    mixed_rows = mixed.transpose(1, 0, 2).reshape(length, local_heads * HEAD_DIM)
    pre_act = jnp.dot(features, full_up, preferred_element_type=jnp.float32) + up_bias
    gelu_rows = gelu_value(pre_act).astype(jnp.bfloat16)
    partial_value = jnp.dot(mixed_rows, full_out, preferred_element_type=jnp.float32) + jnp.dot(
        gelu_rows, full_down, preferred_element_type=jnp.float32
    )
    branch = lax.psum_scatter(partial_value, "tp", scatter_dimension=0, tiled=True)
    layer_output = (own_rows + branch + out_bias + down_bias).astype(jnp.bfloat16)
    grad_rows = lax.all_gather(out_cotangent, "tp", axis=0, tiled=True)
    back_qkv, back_out, back_up, back_down = (full_qkv, full_out, full_up, full_down)
    down_grad = cross_rows(gelu_rows, grad_rows)
    grad_pre = cross_cols(grad_rows, back_down) * gelu_slope(pre_act)
    pre_grads = grad_pre.astype(jnp.bfloat16)
    up_grad = cross_rows(features, pre_grads)
    up_bias_part = jnp.sum(grad_pre, axis=0)
    feature_grad = cross_cols(pre_grads, back_up)
    out_grad = cross_rows(mixed_rows, grad_rows)
    mixed_grad = (
        cross_cols(grad_rows, back_out)
        .astype(jnp.bfloat16)
        .reshape(length, local_heads, HEAD_DIM)
        .transpose(1, 0, 2)
    )

    def backward_head(member):
        return head_backward(
            member[0],
            member[1],
            member[2],
            member[3],
            member[4],
            member[5],
            segment_row,
            score_scale,
        )

    grad_q, grad_k, grad_v = lax.map(
        backward_head, (queries, keys_all, values_all, mixed, mixed_grad, log_total)
    )
    grad_q = unrotate(grad_q.transpose(1, 0, 2), cos_table, sin_table)
    grad_k = unrotate(grad_k.transpose(1, 0, 2), cos_table, sin_table)
    grad_v = grad_v.transpose(1, 0, 2)
    packed_grad = jnp.stack([grad_q, grad_k, grad_v], axis=2).reshape(
        length, 3 * local_heads * HEAD_DIM
    )
    qkv_bias_part = jnp.sum(packed_grad, axis=0)
    packed_bf = packed_grad.astype(jnp.bfloat16)
    qkv_grad = cross_rows(features, packed_bf)
    feature_grad = feature_grad + cross_cols(packed_bf, back_qkv)
    qkv_grad, out_grad, up_grad, down_grad = (
        lax.psum_scatter(qkv_grad, "fsdp", scatter_dimension=0, tiled=True),
        lax.psum_scatter(out_grad, "fsdp", scatter_dimension=1, tiled=True),
        lax.psum_scatter(up_grad, "fsdp", scatter_dimension=0, tiled=True),
        lax.psum_scatter(down_grad, "fsdp", scatter_dimension=1, tiled=True),
    )
    row_grad = lax.psum_scatter(feature_grad, "tp", scatter_dimension=0, tiled=True)
    cot_rows = out_cotangent.astype(jnp.float32)
    gain_grad, shift_grad, bias_grad = lax.psum(
        (jnp.sum(row_grad * normed, axis=0), jnp.sum(row_grad, axis=0), jnp.sum(cot_rows, axis=0)),
        ("fsdp", "tp"),
    )
    qkv_bias_grad, up_bias_grad = lax.psum((qkv_bias_part, up_bias_part), "fsdp")
    scaled = row_grad * norm_gain
    input_grad = (
        cot_rows
        + inverse
        * (
            scaled
            - jnp.mean(scaled, axis=-1, keepdims=True)
            - normed * jnp.mean(scaled * normed, axis=-1, keepdims=True)
        )
    ).astype(jnp.bfloat16)
    return (
        layer_output,
        input_grad,
        gain_grad,
        shift_grad,
        qkv_grad,
        qkv_bias_grad,
        out_grad,
        bias_grad,
        up_grad,
        up_bias_grad,
        down_grad,
        bias_grad,
    )


def solution(mesh):
    in_specs = (
        P(("fsdp", "tp"), None),
        P(("fsdp", "tp"), None),
        P("fsdp", None),
        P(),
        P(),
        P("fsdp", "tp"),
        P("tp"),
        P("tp", "fsdp"),
        P(),
        P("fsdp", "tp"),
        P("tp"),
        P("tp", "fsdp"),
        P(),
    )
    out_specs = (
        P(("fsdp", "tp"), None),
        P(("fsdp", "tp"), None),
        P(),
        P(),
        P("fsdp", "tp"),
        P("tp"),
        P("tp", "fsdp"),
        P(),
        P("fsdp", "tp"),
        P("tp"),
        P("tp", "fsdp"),
        P(),
    )
    return jax.shard_map(body, mesh=mesh, in_specs=in_specs, out_specs=out_specs, check_vma=False)
```

profile of v0, /device:TPU:0, one launch (start us, length us, event | category | flops | bytes accessed | tf_op | source)
XLA Modules:
  0.0 530.0 jit_solution(7264286757015813341)
XLA Ops:
  9.7 2.0 fusion.64
  13.9 34.6 %all_gather.19 = bf16[768,576]{1,0:T(8,128)(2,1)S(1)} all-gather(bf16[96,576]{1,0:T(8,128)(2,1)S(1)} %copy-done.11), channel_id=1, replica_groups=mesh['fsdp'=8,'tp'=4] {'fsdp'}, dimensions={0}, use_global_device_ids=true | all-gather | bytes 995328 | tf_op jit(solution)/shard_map/all_gather | solution.py:165
  49.3 31.3 %all_gather.20 = bf16[192,768]{0,1:T(8,128)(2,1)S(1)} all-gather(bf16[192,96]{0,1:T(8,128)(2,1)S(1)} %copy.81), channel_id=1, replica_groups=mesh['fsdp'=8,'tp'=4] {'fsdp'}, dimensions={1}, use_global_device_ids=true | all-gather | bytes 331776 | tf_op jit(solution)/shard_map/all_gather | solution.py:166
  80.9 2.5 convolution_add_fusion.4
  86.6 16.1 %while.28 = (s32[]{:T(128)}, bf16[3,1024,64]{1,2,0:T(8,128)(2,1)}, f32[3,1024,1]{1,2,0:T(1,128)S(1)}, s32[1024]{0:T(1024)S(1)}, bf16[3,1024,64]{2,1,0:T(8,128)(2...) while((s32[]{:T(128)}, bf16[3,1024,64]{1,2,0:T(8,128)(2,1)}, ...), condition=%wide.region_9.10_spmd, body=%wide.region_4.9_spmd.sunk | while | flops 209518592 | bytes 10947209 | solution.py:183
  88.2 1.8 fusion.151
  93.5 1.8 fusion.151
  98.9 1.8 fusion.151
  102.7 2.1 convolution_convert_fusion.2
  106.0 45.1 %while.29 = (s32[]{:T(128)}, f32[3,1024,64]{1,2,0:T(8,128)}, f32[3,1024,64]{1,2,0:T(8,128)}, f32[3,1024,64]{1,2,0:T(8,128)}, s32[1024]{0:T(1024)S(1)}, /*index=5...) while((s32[]{:T(128)}, f32[3,1024,64]{1,2,0:T(8,128)}, ...), condition=%wide.region_13.14_spmd, body=%wide.region_11.13_spmd.sunk | while | flops 512424960 | bytes 20644056 | solution.py:220
  106.0 1.8 subtract_exponential_fusion.2
  110.1 1.4 multiply_convert_fusion.3
  111.6 1.4 fusion.167
  114.4 2.0 fusion.172
  116.4 1.4 fusion.166
  121.0 1.8 subtract_exponential_fusion.2
  125.2 1.4 multiply_convert_fusion.3
  126.6 1.4 fusion.167
  129.5 2.0 fusion.172
  131.4 1.4 fusion.166
  136.1 1.8 subtract_exponential_fusion.2
  140.2 1.4 multiply_convert_fusion.3
  141.6 1.4 fusion.167
  144.5 2.0 fusion.172
  146.4 1.4 fusion.166
  155.5 1.5 fusion.56
  158.2 2.6 convolution_bitcast_fusion
  161.1 5.4 %multiply_convert_fusion.1 = (bf16[1024,768]{1,0:T(8,128)(2,1)}, f32[1024,768]{1,0:T(8,128)}) fusion(f32[768]{0:T(1024)S(1)} %copy-done.19, bf16[1024,768]{1,0:T(8,128)(2,1)} %all-gather.5.cloned.1.call-done, bf16[768,768]{1,0:T(8,128)(2,1)} %all-gather.7.cloned.1.call-done), kind=kOutput, calls=%fused_computation.93 | convolution fusion | flops 1212678144 | bytes 7474176 | tf_op jit(solution)/shard_map/dot_general | solution.py:185
  166.5 4.1 fusion.91
  170.7 1.4 fusion.76
  172.8 3.1 convolution_add_fusion.2
  176.0 3.2 fusion.92
  179.3 3.3 convolution_add_fusion.3
  182.7 4.5 fusion.93
  187.2 4.8 fusion.74
  192.1 4.3 fusion.94
  196.5 1.4 fusion.55
  197.9 22.1 %all-reduce.3 = (f32[576]{0:T(1024)}, f32[768]{0:T(1024)}) all-reduce(f32[576]{0:T(1024)S(1)} %reduce_sum.120, f32[768]{0:T(1024)S(1)} %get-tuple-element.415), channel_id=1, replica_groups=mesh['fsdp'=8,'tp'=4] {'fsdp'}, use_global_device_ids=true, to_apply=%region_23.24 | all-reduce | flops 1344 | bytes 10752 | tf_op jit(solution)/shard_map/psum | solution.py:245
  220.1 5.1 reduce-scatter.19.cloned.1.call-done
  225.1 1.6 copy.90
  226.8 37.7 %reduce-scatter.11.cloned.1.call-done = f32[256,768]{1,0:T(8,128)} async-done(((f32[1024,768]{1,0:T(8,128)}), f32[256,768]{1,0:T(8,128)}) %reduce-scatter.11.cloned.1.call-update) | async-done | bytes 786448 | tf_op jit(solution)/shard_map/reduce_scatter | solution.py:239
  264.5 1.6 fusion.68
  266.0 38.9 %reduce-scatter.9.cloned.1.call-done = f32[256,768]{1,0:T(8,128)} async-done(((f32[1024,768]{1,0:T(8,128)}), f32[256,768]{1,0:T(8,128)}) %reduce-scatter.9.cloned.1.call-update) | async-done | bytes 786448 | tf_op jit(solution)/shard_map/reduce_scatter | solution.py:190
  304.9 2.6 convert_reduce_fusion.1
  307.6 40.2 %all-reduce.2 = (f32[768]{0:T(1024)}, f32[768]{0:T(1024)}, f32[768]{0:T(1024)S(1)}) all-reduce(f32[768]{0:T(1024)S(1)} %get-tuple-element.331, f32[768]{0:T(1024)S(1)} %get-tuple-element.334, f32[768]{0:T(1024)S(1)} %get-tuple-element.398), channel_id=1, replica_groups=mesh['fsdp'=8,'tp'=4] {'fsdp','tp'}, use_global_device_ids=true, to_apply=%region_18.19 | all-reduce | flops 2304 | bytes 18432 | tf_op jit(solution)/shard_map/psum | solution.py:241
  347.8 28.9 %reduce-scatter.13.cloned.1.call-done = f32[96,576]{1,0:T(8,128)} async-done(((f32[768,576]{1,0:T(8,128)}), f32[96,576]{1,0:T(8,128)}) %reduce-scatter.13.cloned.1.call-update) | async-done | bytes 221200 | tf_op jit(solution)/shard_map/reduce_scatter | solution.py:234
  376.7 73.0 %reduce-scatter.15.cloned.1.call-done = f32[96,768]{1,0:T(8,128)} async-done(((f32[768,768]{1,0:T(8,128)}), f32[96,768]{1,0:T(8,128)}) %reduce-scatter.15.cloned.1.call-update) | async-done | bytes 294928 | tf_op jit(solution)/shard_map/reduce_scatter | solution.py:236
  449.7 72.9 %reduce-scatter.17.cloned.1.call-done = f32[768,96]{0,1:T(8,128)} async-done(((f32[768,768]{0,1:T(8,128)}), f32[768,96]{0,1:T(8,128)}) %reduce-scatter.17.cloned.1.call-update) | async-done | bytes 294928 | tf_op jit(solution)/shard_map/reduce_scatter | solution.py:237
  (194 shorter events, 49.0 us)
Async XLA Ops:
  7.2 6.7 %copy-start.11 = (bf16[96,576]{1,0:T(8,128)(2,1)S(1)}, bf16[96,576]{1,0:T(8,128)(2,1)}, u32[]{:S(2)}) copy-start(bf16[96,576]{1,0:T(8,128)(2,1)} %param.22) | copy-start | bytes 331780
  7.2 41.3 %copy-start.10 = (s32[1,1024]{1,0:T(1,128)S(1)}, s32[1,1024]{1,0:T(1,128)}, u32[]{:S(2)}) copy-start(s32[1,1024]{1,0:T(1,128)} %param.19) | copy-start | bytes 12292
  7.2 42.0 %copy-start.12 = (bf16[192,96]{1,0:T(8,128)(2,1)S(1)}, bf16[192,96]{1,0:T(8,128)(2,1)}, u32[]{:S(2)}) copy-start(bf16[192,96]{1,0:T(8,128)(2,1)} %param.24) | copy-start | bytes 110596
  7.2 73.7 %all-gather.5.cloned.1.call-start = ((), (), s32[]{:S(2)}) async-start(), calls=%async_computation.6 | async-start | bytes 1966080 | tf_op jit(solution)/shard_map/all_gather | solution.py:162
  8.4 72.5 %copy-start.18 = (f32[576]{0:T(1024)S(1)}, f32[576]{0:T(1024)}, u32[]{:S(2)}) copy-start(f32[576]{0:T(1024)} %param.23) | copy-start | bytes 6916
  11.7 91.0 %all-gather.11.cloned.1.call-start = ((), (), s32[]{:S(2)}) async-start(), calls=%async_computation.10 | async-start | bytes 1966080 | tf_op jit(solution)/shard_map/all_gather | solution.py:192
  12.5 148.6 %all-gather.7.cloned.1.call-start = ((), (), s32[]{:S(2)}) async-start(), calls=%async_computation.7 | async-start | bytes 1327104 | tf_op jit(solution)/shard_map/all_gather | solution.py:167
  13.2 153.3 %all-gather.9.cloned.1.call-start = ((), (), s32[]{:S(2)}) async-start(), calls=%async_computation.8 | async-start | bytes 1327104 | tf_op jit(solution)/shard_map/all_gather | solution.py:168
  13.8 211.3 %reduce-scatter.19.cloned.1.call-start = ((), (), s32[]{:S(2)}) async-start(), calls=%async_computation.15 | async-start | bytes 884736
  48.5 35.0 %copy-start.4 = (bf16[768,576]{1,0:T(8,128)(2,1)}, bf16[768,576]{1,0:T(8,128)(2,1)S(1)}, u32[]{:S(2)}) copy-start(bf16[768,576]{1,0:T(8,128)(2,1)S(1)} %all_gather.19) | copy-start | bytes 2654212
  80.6 22.1 %copy-start.6 = (bf16[192,768]{0,1:T(8,128)(2,1)}, bf16[192,768]{0,1:T(8,128)(2,1)S(1)}, u32[]{:S(2)}) copy-start(bf16[192,768]{0,1:T(8,128)(2,1)S(1)} %all_gather.20) | copy-start | bytes 884740
  110.1 2.8 copy-start
  125.1 2.8 copy-start
  140.2 2.8 copy-start
  151.1 2.3 copy-start.9
  155.5 2.6 copy-start.2
  158.2 2.9 copy-start.19
  160.8 103.7 %reduce-scatter.11.cloned.1.call-start = ((), (), s32[]{:S(2)}) async-start(), calls=%async_computation.11 | async-start | bytes 3932160 | tf_op jit(solution)/shard_map/reduce_scatter | solution.py:239
  166.5 4.2 copy-start.17
  170.6 1.5 copy-start.20
  170.7 1.8 copy-start.3
  170.7 2.1 copy-start.5
  175.9 129.0 %reduce-scatter.9.cloned.1.call-start = ((), (), s32[]{:S(2)}) async-start(), calls=%async_computation.9 | async-start | bytes 3932160 | tf_op jit(solution)/shard_map/reduce_scatter | solution.py:190
  176.0 3.2 copy-start.7
  182.6 194.1 %reduce-scatter.13.cloned.1.call-start = ((), (), s32[]{:S(2)}) async-start(), calls=%async_computation.12 | async-start | bytes 2211840 | tf_op jit(solution)/shard_map/reduce_scatter | solution.py:234
  187.2 262.5 %reduce-scatter.15.cloned.1.call-start = ((), (), s32[]{:S(2)}) async-start(), calls=%async_computation.13 | async-start | bytes 2654208 | tf_op jit(solution)/shard_map/reduce_scatter | solution.py:236
  192.0 330.5 %reduce-scatter.17.cloned.1.call-start = ((), (), s32[]{:S(2)}) async-start(), calls=%async_computation.14 | async-start | bytes 2654208 | tf_op jit(solution)/shard_map/reduce_scatter | solution.py:237
  196.4 68.1 %copy-start.1 = (bf16[256,768]{1,0:T(8,128)(2,1)S(1)}, bf16[256,768]{1,0:T(8,128)(2,1)}, u32[]{:S(2)}) copy-start(bf16[256,768]{1,0:T(8,128)(2,1)} %param.17) | copy-start | bytes 1179652
  196.4 68.1 %copy-start.13 = (f32[768]{0:T(1024)S(1)}, f32[768]{0:T(1024)}, u32[]{:S(2)}) copy-start(f32[768]{0:T(1024)} %param.20) | copy-start | bytes 9220
  196.4 108.5 %copy-start.8 = (bf16[256,768]{1,0:T(8,128)(2,1)S(1)}, bf16[256,768]{1,0:T(8,128)(2,1)}, u32[]{:S(2)}) copy-start(bf16[256,768]{1,0:T(8,128)(2,1)} %param.18) | copy-start | bytes 1179652
  196.4 108.5 %copy-start.14 = (f32[768]{0:T(1024)S(1)}, f32[768]{0:T(1024)}, u32[]{:S(2)}) copy-start(f32[768]{0:T(1024)} %param.29) | copy-start | bytes 9220
  196.5 108.5 %copy-start.15 = (f32[768]{0:T(1024)S(1)}, f32[768]{0:T(1024)}, u32[]{:S(2)}) copy-start(f32[768]{0:T(1024)} %param.25) | copy-start | bytes 9220
  347.8 175.4 %copy-start.16 = (f32[768]{0:T(1024)}, f32[768]{0:T(1024)S(1)}, u32[]{:S(2)}) copy-start(f32[768]{0:T(1024)S(1)} %get-tuple-element.670) | copy-start | bytes 9220
Sparse Core Ops, SparseCore 0:
  11.8 22.3 all-gather.4
  35.8 19.6 all-gather.10
  57.7 41.2 all-gather.6
  101.0 40.0 all-gather.8
  160.9 64.1 reduce-scatter.18
  227.5 36.8 reduce-scatter.10
  267.0 37.8 reduce-scatter.8
  309.0 67.6 reduce-scatter.12
  380.8 68.8 reduce-scatter.14
  453.6 68.9 reduce-scatter.16
where the time goes:
time: 531 us; the launch traced here: 530 us
  waiting for transfers between devices  258 us (49%)
  blocking collectives  128 us (24%)
  matrix products  89.1 us (17%)
  other arithmetic  24.5 us (5%)
  between operations  14.6 us (3%)
  local copies, waits for them, and re-layouts  14.2 us (3%)
    reduce_scatter x1, waiting for transfers between devices, body(): lax.psum_scatter(up_grad, 'fsdp', scatter_dimension=0, tiled=True)  73 us
    reduce_scatter x1, waiting for transfers between devices, body(): lax.psum_scatter(down_grad, 'fsdp', scatter_dimension=1, tiled=True)  72.9 us
    psum x1, blocking collectives, body(): lax.psum((jnp.sum(row_grad * normed, axis=0), jnp.sum(row_grad, axis=0),...  40.2 us
    reduce_scatter x1, waiting for transfers between devices, body(): lax.psum_scatter(partial_value, 'tp', scatter_dimension=0, tiled=True)  38.9 us
    reduce_scatter x1, waiting for transfers between devices, body(): lax.psum_scatter(feature_grad, 'tp', scatter_dimension=0, tiled=True)  37.7 us
    dot_general x22, matrix products, cross_cols(): lax.dot_general(left, right, (((1,), (1,)), ((), ())), preferred_element_...  34.8 us
    all_gather x1, blocking collectives, body(): lax.all_gather(qkv_weight, 'fsdp', axis=0, tiled=True)  34.6 us
    all_gather x1, blocking collectives, body(): lax.all_gather(out_weight, 'fsdp', axis=1, tiled=True)  31.3 us
  transfers between devices with their start and end apart: 10, of which 6 were waited for; matrix products, arithmetic and copies ran while one was open for 23% of the time, Pallas kernels for 0%

commit v1 on v0

--- a/solution.py
+++ b/solution.py
@@ -7,6 +7,22 @@
 ROT = 16
 EPSILON = 1e-05
 ROTARY_BASE = 10000.0
+
+
+def keep_up_stacks_all(content):
+    which_axis = "fsdp"
+    x_new, z2, plain = (lax.axis_size(which_axis), lax.axis_index(which_axis), content.shape[1])
+    arr_out, u_next = (content, 1)
+    while u_next < x_new:
+        blocks_here = []
+        for c in tuple(range(x_new)):
+            blocks_here.append((c, (c - u_next) % x_new))
+        arr_out = jnp.concatenate(
+            [arr_out, lax.ppermute(arr_out, axis_name=which_axis, perm=blocks_here)], 1
+        )
+        u_next = 2 * u_next
+    block_out = jnp.roll(arr_out, z2 * plain, 1)
+    return block_out
 
 
 def layer_norm(values, gain, shift):
@@ -163,7 +179,7 @@
     length = features.shape[0]
     full_qkv, full_out, full_up, full_down = (
         lax.all_gather(qkv_weight, "fsdp", axis=0, tiled=True),
-        lax.all_gather(out_weight, "fsdp", axis=1, tiled=True),
+        keep_up_stacks_all(out_weight),
         lax.all_gather(up_weight, "fsdp", axis=0, tiled=True),
         lax.all_gather(down_weight, "fsdp", axis=1, tiled=True),
     )

time: 531 us -> 514 us (0.968)
  blocking collectives: 128 us -> 91.5 us
  waiting for transfers between devices: 258 us -> 270 us
  starting transfers between devices: 0.58 us -> 7.36 us
    all_gather x1 -> x0, blocking collectives: 31.3 us -> none  [body(): lax.all_gather(out_weight, 'fsdp', axis=1, tiled=True)]
    ppermute x0 -> x3, waiting for transfers between devices: none -> 11.6 us  [keep_up_stacks_all(): lax.ppermute(arr_out, axis_name=which_axis, perm=blocks_here)]
    ppermute x0 -> x3, starting transfers between devices: none -> 6.77 us  [keep_up_stacks_all(): lax.ppermute(arr_out, axis_name=which_axis, perm=blocks_here)]
  transfers between devices with their start and end apart: 10 -> 13, of which waited for: 6 -> 8; matrix products, arithmetic and copies ran while one was open for 23% -> 24% of each run, Pallas kernels for 0% -> 0%
where the time goes in v1:
time: 514 us; the launch traced here: 513 us
  waiting for transfers between devices  270 us (53%)
  blocking collectives  91.5 us (18%)
  matrix products  89.4 us (17%)
  other arithmetic  24.7 us (5%)
  between operations  14.7 us (3%)
  local copies, waits for them, and re-layouts  14.5 us (3%)
  starting transfers between devices  7.36 us (1%)
    reduce_scatter x1, waiting for transfers between devices, body(): lax.psum_scatter(down_grad, 'fsdp', scatter_dimension=1, tiled=True)  72.8 us
    reduce_scatter x1, waiting for transfers between devices, body(): lax.psum_scatter(up_grad, 'fsdp', scatter_dimension=0, tiled=True)  72.8 us
    psum x1, blocking collectives, body(): lax.psum((jnp.sum(row_grad * normed, axis=0), jnp.sum(row_grad, axis=0),...  40.2 us
    reduce_scatter x1, waiting for transfers between devices, body(): lax.psum_scatter(partial_value, 'tp', scatter_dimension=0, tiled=True)  38.9 us
    reduce_scatter x1, waiting for transfers between devices, body(): lax.psum_scatter(feature_grad, 'tp', scatter_dimension=0, tiled=True)  37.6 us
    dot_general x22, matrix products, cross_cols(): lax.dot_general(left, right, (((1,), (1,)), ((), ())), preferred_element_...  34.8 us
    all_gather x1, blocking collectives, body(): lax.all_gather(qkv_weight, 'fsdp', axis=0, tiled=True)  32.7 us
    reduce_scatter x1, waiting for transfers between devices, body(): lax.psum_scatter(qkv_grad, 'fsdp', scatter_dimension=0, tiled=True)  28.9 us
  transfers between devices with their start and end apart: 13, of which 8 were waited for; matrix products, arithmetic and copies ran while one was open for 24% of the time, Pallas kernels for 0%

profile of v1, /device:TPU:0, one launch (start us, length us, event | category | flops | bytes accessed | tf_op | source)
XLA Modules:
  0.0 512.5 jit_solution(12695177688361902886)
XLA Ops:
  9.7 2.0 fusion.64
  13.3 6.1 %collective-permute-start = (bf16[192,96]{1,0:T(8,128)(2,1)S(1)}, bf16[192,96]{1,0:T(8,128)(2,1)S(1)}, u32[]{:S(2)}, u32[]{:S(2)}) collective-permute-start(bf16[192,96]{1,0:T(8,128)(2,1)S(1)} %copy-done.10), channel_id=1, source_target_pairs={{0,28},{4,0},{8,4},{12,8},{16,12},{20,16},{24,20},{28,24},{1,29},{... | collective-permute-start | bytes 110600 | tf_op jit(solution)/shard_map/ppermute | solution.py:21
  19.4 32.7 %all_gather.16 = bf16[768,576]{1,0:T(8,128)(2,1)S(1)} all-gather(bf16[96,576]{1,0:T(8,128)(2,1)S(1)} %copy-done.12), channel_id=1, replica_groups=mesh['fsdp'=8,'tp'=4] {'fsdp'}, dimensions={0}, use_global_device_ids=true | all-gather | bytes 995328 | tf_op jit(solution)/shard_map/all_gather | solution.py:181
  53.6 5.1 collective-permute-done.1
  59.2 6.5 %collective-permute-done.2 = bf16[192,384]{1,0:T(8,128)(2,1)S(1)} collective-permute-done((bf16[192,384]{1,0:T(8,128)(2,1)S(1)}, bf16[192,384]{1,0:T(8,128)(2,1)S(1)}, u32[]{:S(2)}, u32[]{:S(2)}) %collective-permute-start.2) | collective-permute-done | bytes 147488 | tf_op jit(solution)/shard_map/ppermute | solution.py:21
  66.1 2.7 convolution_add_fusion.4
  72.0 16.1 %while.28 = (s32[]{:T(128)}, bf16[3,1024,64]{1,2,0:T(8,128)(2,1)}, f32[3,1024,1]{1,2,0:T(1,128)S(1)}, s32[1024]{0:T(1024)S(1)}, bf16[3,1024,64]{2,1,0:T(8,128)(2...) while((s32[]{:T(128)}, bf16[3,1024,64]{1,2,0:T(8,128)(2,1)}, ...), condition=%wide.region_9.10_spmd, body=%wide.region_4.9_spmd.sunk | while | flops 209518592 | bytes 10947209 | solution.py:199
  73.6 1.8 fusion.153
  78.9 1.8 fusion.153
  84.3 1.7 fusion.153
  88.1 2.1 convolution_convert_fusion.2
  91.4 45.1 %while.29 = (s32[]{:T(128)}, f32[3,1024,64]{1,2,0:T(8,128)}, f32[3,1024,64]{1,2,0:T(8,128)}, f32[3,1024,64]{1,2,0:T(8,128)}, s32[1024]{0:T(1024)S(1)}, /*index=5...) while((s32[]{:T(128)}, f32[3,1024,64]{1,2,0:T(8,128)}, ...), condition=%wide.region_13.14_spmd, body=%wide.region_11.13_spmd.sunk | while | flops 512424960 | bytes 20644056 | solution.py:236
  91.4 1.8 subtract_exponential_fusion.2
  95.5 1.4 multiply_convert_fusion.3
  99.8 2.0 fusion.174
  101.8 1.4 fusion.168
  106.4 1.8 subtract_exponential_fusion.2
  110.5 1.4 multiply_convert_fusion.3
  114.8 2.0 fusion.174
  116.8 1.4 fusion.168
  121.4 1.8 subtract_exponential_fusion.2
  125.6 1.4 multiply_convert_fusion.3
  127.0 1.4 fusion.169
  129.9 2.0 fusion.174
  131.8 1.4 fusion.168
  140.9 1.5 fusion.56
  143.5 2.6 convolution_bitcast_fusion
  146.5 5.5 %multiply_convert_fusion.1 = (bf16[1024,768]{1,0:T(8,128)(2,1)}, f32[1024,768]{1,0:T(8,128)}) fusion(f32[768]{0:T(1024)S(1)} %copy-done.19, bf16[1024,768]{1,0:T(8,128)(2,1)} %all-gather.5.cloned.1.call-done, bf16[768,768]{1,0:T(8,128)(2,1)} %all-gather.7.cloned.1.call-done), kind=kOutput, calls=%fused_computation.93 | convolution fusion | flops 1212678144 | bytes 7474176 | tf_op jit(solution)/shard_map/dot_general | solution.py:201
  151.9 4.1 fusion.95
  156.1 1.4 fusion.76
  158.2 3.1 convolution_add_fusion.2
  161.4 3.2 fusion.96
  164.7 3.5 convolution_add_fusion.3
  168.2 4.5 fusion.97
  172.8 4.8 fusion.74
  177.6 4.3 fusion.98
  182.0 1.4 fusion.55
  183.5 18.7 %all-reduce.3 = (f32[576]{0:T(1024)}, f32[768]{0:T(1024)}) all-reduce(f32[576]{0:T(1024)S(1)} %reduce_sum.120, f32[768]{0:T(1024)S(1)} %get-tuple-element.415), channel_id=1, replica_groups=mesh['fsdp'=8,'tp'=4] {'fsdp'}, use_global_device_ids=true, to_apply=%region_23.24 | all-reduce | flops 1344 | bytes 10752 | tf_op jit(solution)/shard_map/psum | solution.py:261
  202.1 5.9 %reduce-scatter.19.cloned.1.call-done = f32[96,192]{1,0:T(8,128)} async-done(((f32[768,192]{1,0:T(8,128)}), f32[96,192]{1,0:T(8,128)}) %reduce-scatter.19.cloned.1.call-update) | async-done | bytes 73744
  208.1 1.6 copy.86
  209.7 37.6 %reduce-scatter.11.cloned.1.call-done = f32[256,768]{1,0:T(8,128)} async-done(((f32[1024,768]{1,0:T(8,128)}), f32[256,768]{1,0:T(8,128)}) %reduce-scatter.11.cloned.1.call-update) | async-done | bytes 786448 | tf_op jit(solution)/shard_map/reduce_scatter | solution.py:255
  247.4 1.6 fusion.68
  248.9 38.9 %reduce-scatter.9.cloned.1.call-done = f32[256,768]{1,0:T(8,128)} async-done(((f32[1024,768]{1,0:T(8,128)}), f32[256,768]{1,0:T(8,128)}) %reduce-scatter.9.cloned.1.call-update) | async-done | bytes 786448 | tf_op jit(solution)/shard_map/reduce_scatter | solution.py:206
  287.8 2.6 convert_reduce_fusion.1
  290.5 40.2 %all-reduce.2 = (f32[768]{0:T(1024)}, f32[768]{0:T(1024)}, f32[768]{0:T(1024)S(1)}) all-reduce(f32[768]{0:T(1024)S(1)} %get-tuple-element.331, f32[768]{0:T(1024)S(1)} %get-tuple-element.334, f32[768]{0:T(1024)S(1)} %get-tuple-element.398), channel_id=1, replica_groups=mesh['fsdp'=8,'tp'=4] {'fsdp','tp'}, use_global_device_ids=true, to_apply=%region_18.19 | all-reduce | flops 2304 | bytes 18432 | tf_op jit(solution)/shard_map/psum | solution.py:257
  330.6 28.9 %reduce-scatter.13.cloned.1.call-done = f32[96,576]{1,0:T(8,128)} async-done(((f32[768,576]{1,0:T(8,128)}), f32[96,576]{1,0:T(8,128)}) %reduce-scatter.13.cloned.1.call-update) | async-done | bytes 221200 | tf_op jit(solution)/shard_map/reduce_scatter | solution.py:250
  359.5 72.8 %reduce-scatter.15.cloned.1.call-done = f32[96,768]{1,0:T(8,128)} async-done(((f32[768,768]{1,0:T(8,128)}), f32[96,768]{1,0:T(8,128)}) %reduce-scatter.15.cloned.1.call-update) | async-done | bytes 294928 | tf_op jit(solution)/shard_map/reduce_scatter | solution.py:252
  432.3 72.8 %reduce-scatter.17.cloned.1.call-done = f32[768,96]{0,1:T(8,128)} async-done(((f32[768,768]{0,1:T(8,128)}), f32[768,96]{0,1:T(8,128)}) %reduce-scatter.17.cloned.1.call-update) | async-done | bytes 294928 | tf_op jit(solution)/shard_map/reduce_scatter | solution.py:253
  (201 shorter events, 52.4 us)
Async XLA Ops:
  7.2 6.1 %copy-start.10 = (bf16[192,96]{1,0:T(8,128)(2,1)S(1)}, bf16[192,96]{1,0:T(8,128)(2,1)}, u32[]{:S(2)}) copy-start(bf16[192,96]{1,0:T(8,128)(2,1)} %param.24) | copy-start | bytes 110596
  7.2 12.2 %copy-start.12 = (bf16[96,576]{1,0:T(8,128)(2,1)S(1)}, bf16[96,576]{1,0:T(8,128)(2,1)}, u32[]{:S(2)}) copy-start(bf16[96,576]{1,0:T(8,128)(2,1)} %param.22) | copy-start | bytes 331780
  7.2 44.9 %copy-start.11 = (s32[1,1024]{1,0:T(1,128)S(1)}, s32[1,1024]{1,0:T(1,128)}, u32[]{:S(2)}) copy-start(s32[1,1024]{1,0:T(1,128)} %param.19) | copy-start | bytes 12292
  7.2 58.9 %all-gather.5.cloned.1.call-start = ((), (), s32[]{:S(2)}) async-start(), calls=%async_computation.6 | async-start | bytes 1966080 | tf_op jit(solution)/shard_map/all_gather | solution.py:178
  11.7 54.4 %copy-start.18 = (f32[576]{0:T(1024)S(1)}, f32[576]{0:T(1024)}, u32[]{:S(2)}) copy-start(f32[576]{0:T(1024)} %param.23) | copy-start | bytes 6916
  11.7 76.4 %all-gather.11.cloned.1.call-start = ((), (), s32[]{:S(2)}) async-start(), calls=%async_computation.10 | async-start | bytes 1966080 | tf_op jit(solution)/shard_map/all_gather | solution.py:208
  12.5 134.0 %all-gather.7.cloned.1.call-start = ((), (), s32[]{:S(2)}) async-start(), calls=%async_computation.7 | async-start | bytes 1327104 | tf_op jit(solution)/shard_map/all_gather | solution.py:183
  13.2 138.7 %all-gather.9.cloned.1.call-start = ((), (), s32[]{:S(2)}) async-start(), calls=%async_computation.8 | async-start | bytes 1327104 | tf_op jit(solution)/shard_map/all_gather | solution.py:184
  13.3 39.6 %collective-permute-start = (bf16[192,96]{1,0:T(8,128)(2,1)S(1)}, bf16[192,96]{1,0:T(8,128)(2,1)S(1)}, u32[]{:S(2)}, u32[]{:S(2)}) collective-permute-start(bf16[192,96]{1,0:T(8,128)(2,1)S(1)} %copy-done.10), channel_id=1, source_target_pairs={{0,28},{4,0},{8,4},{12,8},{16,12},{20,16},{24,20},{28,24},{1,29},{... | collective-permute-start | bytes 110600 | tf_op jit(solution)/shard_map/ppermute | solution.py:21
  19.4 188.7 %reduce-scatter.19.cloned.1.call-start = ((), (), s32[]{:S(2)}) async-start(), calls=%async_computation.15 | async-start | bytes 884736
  52.1 16.7 %copy-start.4 = (bf16[768,576]{1,0:T(8,128)(2,1)}, bf16[768,576]{1,0:T(8,128)(2,1)S(1)}, u32[]{:S(2)}) copy-start(bf16[768,576]{1,0:T(8,128)(2,1)S(1)} %all_gather.16) | copy-start | bytes 2654212
  53.0 5.7 %collective-permute-start.1 = (bf16[192,192]{1,0:T(8,128)(2,1)S(1)}, bf16[192,192]{1,0:T(8,128)(2,1)S(1)}, u32[]{:S(2)}, u32[]{:S(2)}) collective-permute-start(bf16[192,192]{1,0:T(8,128)(2,1)S(1)} %pad_maximum_fusion.2), channel_id=1, source_target_pairs={{0,24},{4,28},{8,0},{12,4},{16,8},{20,12},{24,16},{28,20},{1,25},{... | collective-permute-start | bytes 221192 | tf_op jit(solution)/shard_map/ppermute | solution.py:21
  58.8 6.9 %collective-permute-start.2 = (bf16[192,384]{1,0:T(8,128)(2,1)S(1)}, bf16[192,384]{1,0:T(8,128)(2,1)S(1)}, u32[]{:S(2)}, u32[]{:S(2)}) collective-permute-start(bf16[192,384]{1,0:T(8,128)(2,1)S(1)} %pad_maximum_fusion.1), channel_id=1, source_target_pairs={{0,16},{4,20},{8,24},{12,28},{16,0},{20,4},{24,8},{28,12},{1,17},{... | collective-permute-start | bytes 442376 | tf_op jit(solution)/shard_map/ppermute | solution.py:21
  66.1 22.1 %copy-start.6 = (bf16[192,1536]{1,0:T(8,128)(2,1)}, bf16[192,1536]{1,0:T(8,128)(2,1)S(1)}, u32[]{:S(2)}) copy-start(bf16[192,1536]{1,0:T(8,128)(2,1)S(1)} %concatenate.73) | copy-start | bytes 1769476
  95.5 2.8 copy-start
  110.5 2.8 copy-start
  125.6 2.8 copy-start
  136.5 2.3 copy-start.9
  140.9 2.6 copy-start.2
  143.5 2.9 copy-start.19
  146.2 101.2 %reduce-scatter.11.cloned.1.call-start = ((), (), s32[]{:S(2)}) async-start(), calls=%async_computation.11 | async-start | bytes 3932160 | tf_op jit(solution)/shard_map/reduce_scatter | solution.py:255
  151.9 4.2 copy-start.17
  156.1 1.5 copy-start.20
  156.1 1.8 copy-start.3
  156.1 2.1 copy-start.5
  161.4 126.4 %reduce-scatter.9.cloned.1.call-start = ((), (), s32[]{:S(2)}) async-start(), calls=%async_computation.9 | async-start | bytes 3932160 | tf_op jit(solution)/shard_map/reduce_scatter | solution.py:206
  161.4 3.2 copy-start.7
  168.2 191.4 %reduce-scatter.13.cloned.1.call-start = ((), (), s32[]{:S(2)}) async-start(), calls=%async_computation.12 | async-start | bytes 2211840 | tf_op jit(solution)/shard_map/reduce_scatter | solution.py:250
  172.7 259.6 %reduce-scatter.15.cloned.1.call-start = ((), (), s32[]{:S(2)}) async-start(), calls=%async_computation.13 | async-start | bytes 2654208 | tf_op jit(solution)/shard_map/reduce_scatter | solution.py:252
  177.5 327.5 %reduce-scatter.17.cloned.1.call-start = ((), (), s32[]{:S(2)}) async-start(), calls=%async_computation.14 | async-start | bytes 2654208 | tf_op jit(solution)/shard_map/reduce_scatter | solution.py:253
  181.9 65.4 %copy-start.1 = (bf16[256,768]{1,0:T(8,128)(2,1)S(1)}, bf16[256,768]{1,0:T(8,128)(2,1)}, u32[]{:S(2)}) copy-start(bf16[256,768]{1,0:T(8,128)(2,1)} %param.17) | copy-start | bytes 1179652
  181.9 65.4 %copy-start.13 = (f32[768]{0:T(1024)S(1)}, f32[768]{0:T(1024)}, u32[]{:S(2)}) copy-start(f32[768]{0:T(1024)} %param.20) | copy-start | bytes 9220
  182.0 105.9 %copy-start.8 = (bf16[256,768]{1,0:T(8,128)(2,1)S(1)}, bf16[256,768]{1,0:T(8,128)(2,1)}, u32[]{:S(2)}) copy-start(bf16[256,768]{1,0:T(8,128)(2,1)} %param.18) | copy-start | bytes 1179652
  182.0 105.8 %copy-start.14 = (f32[768]{0:T(1024)S(1)}, f32[768]{0:T(1024)}, u32[]{:S(2)}) copy-start(f32[768]{0:T(1024)} %param.29) | copy-start | bytes 9220
  182.0 105.8 %copy-start.15 = (f32[768]{0:T(1024)S(1)}, f32[768]{0:T(1024)}, u32[]{:S(2)}) copy-start(f32[768]{0:T(1024)} %param.25) | copy-start | bytes 9220
  330.6 175.1 %copy-start.16 = (f32[768]{0:T(1024)}, f32[768]{0:T(1024)S(1)}, u32[]{:S(2)}) copy-start(f32[768]{0:T(1024)S(1)} %get-tuple-element.670) | copy-start | bytes 9220
Sparse Core Ops, SparseCore 0:
  11.8 22.3 all-gather.4
  35.8 19.6 all-gather.10
  57.6 41.1 all-gather.6
  100.9 39.8 all-gather.8
  146.3 61.7 reduce-scatter.18
  210.5 36.8 reduce-scatter.10
  249.9 37.8 reduce-scatter.8
  291.9 67.6 reduce-scatter.12
  363.6 68.6 reduce-scatter.14
  436.2 68.8 reduce-scatter.16
